TPU v7x, 32 devices: a whole 2x2x4 slice. The times are simulated.
32 devices in a mesh: dp: 16 (over z, y, core), ctx: 2 (over x).
Axes of the slice: x: 2, y: 2, z: 4, core: 2. Of those that a mesh axis runs over, the one named last changes fastest.
Arguments:
- tokens: bfloat16 [32, 1024, 768], P('dp', 'ctx'), may hold values from -6 to 6
- out_grad: bfloat16 [32, 1024, 768], P('dp', 'ctx'), may hold values from -6 to 6
- logit_grad: float32 [32, 14], P('dp'), may hold values from -6 to 6
- piece_start: int32 [32, 2], P('dp'), may hold values from 0 to 960, as said below
- piece_len: int32 [32, 2], P('dp'), may hold values from 64 to 256, as said below
- qkv_weight: bfloat16 [768, 2304], P(('dp', 'ctx')), may hold values from -0.21875 to 0.21875
- query_bias: bfloat16 [768], P(('dp', 'ctx')), may hold values from -3 to 3
- value_bias: bfloat16 [768], P(('dp', 'ctx')), may hold values from -3 to 3
- out_weight: bfloat16 [768, 768], P(('dp', 'ctx')), may hold values from -0.875 to 0.875
- out_bias: bfloat16 [768], P(('dp', 'ctx')), may hold values from -3 to 3
- gain_one: bfloat16 [768], P(('dp', 'ctx')), may hold values from 0.5 to 1.5
- shift_one: bfloat16 [768], P(('dp', 'ctx')), may hold values from -3 to 3
- in_weight: bfloat16 [768, 3072], P(('dp', 'ctx')), may hold values from -0.21875 to 0.21875
- in_bias: bfloat16 [3072], P(('dp', 'ctx')), may hold values from -3 to 3
- back_weight: bfloat16 [3072, 768], P(('dp', 'ctx')), may hold values from -0.109375 to 0.109375
- back_bias: bfloat16 [768], P(('dp', 'ctx')), may hold values from -3 to 3
- gain_two: bfloat16 [768], P(('dp', 'ctx')), may hold values from 0.5 to 1.5
- shift_two: bfloat16 [768], P(('dp', 'ctx')), may hold values from -3 to 3
- reduce_weight: bfloat16 [768, 128], P(('dp', 'ctx')), may hold values from -0.21875 to 0.21875
- reduce_bias: bfloat16 [128], replicated, may hold values from -3 to 3
- pool_query: bfloat16 [128], replicated, may hold values from -16 to 16
- pool_weight: bfloat16 [128, 128], replicated, may hold values from -1 to 1
- pool_bias: bfloat16 [128], replicated, may hold values from -3 to 3
- class_weight: bfloat16 [128, 14], replicated, may hold values from -0.5 to 0.5
- class_bias: bfloat16 [14], replicated, may hold values from -6 to 6
Outputs:
- layer_out: bfloat16 [32, 1024, 768], P('dp', 'ctx')
- logits: float32 [32, 14], P('dp')
- token_grad: bfloat16 [32, 1024, 768], P('dp', 'ctx')
- qkv_weight_grad: float32 [768, 2304], P(('dp', 'ctx'))
- query_bias_grad: float32 [768], P(('dp', 'ctx'))
- value_bias_grad: float32 [768], P(('dp', 'ctx'))
- out_weight_grad: float32 [768, 768], P(('dp', 'ctx'))
- out_bias_grad: float32 [768], P(('dp', 'ctx'))
- gain_one_grad: float32 [768], P(('dp', 'ctx'))
- shift_one_grad: float32 [768], P(('dp', 'ctx'))
- in_weight_grad: float32 [768, 3072], P(('dp', 'ctx'))
- in_bias_grad: float32 [3072], P(('dp', 'ctx'))
- back_weight_grad: float32 [3072, 768], P(('dp', 'ctx'))
- back_bias_grad: float32 [768], P(('dp', 'ctx'))
- gain_two_grad: float32 [768], P(('dp', 'ctx'))
- shift_two_grad: float32 [768], P(('dp', 'ctx'))
- reduce_weight_grad: float32 [768, 128], P(('dp', 'ctx'))
- reduce_bias_grad: float32 [128], replicated
- pool_query_grad: float32 [128], replicated
- pool_weight_grad: float32 [128, 128], replicated
- pool_bias_grad: float32 [128], replicated
- class_weight_grad: float32 [128, 14], replicated
- class_bias_grad: float32 [14], replicated
Inputs may be any that keep to these rules, and one draw needn't show every extreme that they name: `piece_len`: each sequence has 2 picture pieces; the first is exactly 256 tokens long. `piece_start`: piece k of a sequence lies wholly within positions k * 512 to (k + 1) * 512 - 1, so pieces never intersect.
All inputs are finite; a program needn't handle non-finite values.
Results may differ from a plain program's by a relative error of at most 0.017.
The roundings to bfloat16 on the way count: a program that leaves them out, or rounds other values in their place, can miss the bound.
Values may be sent and summed in bfloat16 or wider, within the bound.
No kernel may reach another device: no remote copies, remote signals or barrier semaphores. Data moves between devices by JAX's collectives and lax.ppermute only.
A program may use at most 256 MiB of HBM per device.

v0:
```python
from functools import partial

import jax
import jax.numpy as jnp
from jax import lax
from jax.sharding import PartitionSpec as P

H = 12
HD = 64
RED = 128
PH = 2
CLS = 14


negative = -1e30
epsilon = 1e-06
highest = lax.Precision.HIGHEST


def joined(value, axis, combine):
    everything = jax.tree.map(lambda part: lax.all_gather(part, axis), value)
    first = jax.tree.map(lambda part: part[0], everything)

    def turn(k, so_far):
        return combine(so_far, jax.tree.map(lambda part: part[k], everything))

    return lax.fori_loop(1, lax.axis_size(axis), turn, first)


def norm_rows(hidden, gain, shift):
    average = jnp.mean(hidden, axis=-1, keepdims=True)
    centred = hidden - average
    inv_std = lax.rsqrt(jnp.mean(centred * centred, axis=-1, keepdims=True) + epsilon)
    normed = centred * inv_std
    return (normed * gain + shift, normed, inv_std)


def norm_back(upstream, normed, inv_std, gain):
    scaled = upstream * gain
    first_mean = jnp.mean(scaled, axis=-1, keepdims=True)
    second = jnp.mean(scaled * normed, axis=-1, keepdims=True)
    return inv_std * (scaled - first_mean - normed * second)


def rows_product(left, right, precision=None):
    return lax.dot_general(
        left,
        right,
        (((0,), (0,)), ((), ())),
        precision=precision,
        preferred_element_type=jnp.float32,
    )


def right_transposed(left, right, precision=None):
    return lax.dot_general(
        left,
        right,
        (((1,), (1,)), ((), ())),
        precision=precision,
        preferred_element_type=jnp.float32,
    )


def piece_labels(positions, starts, lengths):
    inside = (positions[None, :, None] >= starts[:, None, :]) & (
        positions[None, :, None] < (starts + lengths)[:, None, :]
    )
    labels = jnp.arange(1, starts.shape[1] + 1, dtype=jnp.int32)
    return jnp.sum(jnp.where(inside, labels, 0), axis=2) - 1


def allowed_pairs(query_pos, key_pos, starts, lengths):
    query_label = piece_labels(query_pos, starts, lengths)
    key_label = piece_labels(key_pos, starts, lengths)
    causal = key_pos[None, None, :] <= query_pos[None, :, None]
    together = (query_label[:, :, None] == key_label[:, None, :]) & (query_label[:, :, None] >= 0)
    return (causal | together)[:, None]


def scores_of(queries, keys, allowed):
    raw_scores = (
        jnp.einsum("gqhe,gkhe->ghqk", queries, keys, preferred_element_type=jnp.float32) * 0.125
    )
    return jnp.where(allowed, raw_scores, negative)


def attend_block(query_pos, key_pos, inputs):
    queries, keys, values, starts, lengths = inputs
    scores = scores_of(queries, keys, allowed_pairs(query_pos, key_pos, starts, lengths))
    row_top = jnp.max(scores, axis=-1, keepdims=True)
    row_total = jnp.sum(jnp.exp(scores - row_top), axis=-1, keepdims=True)
    log_total = row_top + jnp.log(row_total)
    prob_low = jnp.exp(scores - log_total).astype(jnp.bfloat16)
    mixed_block = jnp.einsum(
        "ghqk,gkhe->gqhe", prob_low, values, preferred_element_type=jnp.float32
    )
    return (mixed_block.astype(jnp.bfloat16), log_total[..., 0])


def score_grads(
    query_pos, key_pos, queries, keys, values, starts, lengths, log_total, grad_mixed, centre
):
    scores = scores_of(queries, keys, allowed_pairs(query_pos, key_pos, starts, lengths))
    prob_full = jnp.exp(scores - log_total[..., None])
    grad_probs = jnp.einsum(
        "gqhe,gkhe->ghqk", grad_mixed, values, preferred_element_type=jnp.float32
    )
    centre = jnp.sum(prob_full * grad_probs, axis=-1)
    grad_scores = (prob_full * (grad_probs - centre[..., None]) * 0.125).astype(jnp.bfloat16)
    return (prob_full, grad_scores, centre)


def attend_back(query_pos, key_pos, inputs):
    queries, keys, values, starts, lengths, log_total, grad_mixed = inputs
    prob_full, grad_scores, centre = score_grads(
        query_pos, key_pos, queries, keys, values, starts, lengths, log_total, grad_mixed, None
    )
    grad_queries = jnp.einsum(
        "ghqk,gkhe->gqhe", grad_scores, keys, preferred_element_type=jnp.float32
    )
    grad_keys = jnp.einsum(
        "ghqk,gqhe->gkhe", grad_scores, queries, preferred_element_type=jnp.float32
    )
    grad_values = jnp.einsum(
        "ghqk,gqhe->gkhe",
        prob_full.astype(jnp.bfloat16),
        grad_mixed,
        preferred_element_type=jnp.float32,
    )
    return (grad_queries, grad_keys, grad_values)


def join_stats(earlier, later):
    joint_top = jnp.maximum(earlier[0], later[0])
    scale_a = jnp.exp(earlier[0] - joint_top)
    scale_b = jnp.exp(later[0] - joint_top)
    repeat = earlier[2].shape[1] // scale_a.shape[1]
    wide_a = jnp.repeat(scale_a, repeat, axis=1)
    wide_b = jnp.repeat(scale_b, repeat, axis=1)
    return (
        joint_top,
        earlier[1] * scale_a + later[1] * scale_b,
        earlier[2] * wide_a + later[2] * wide_b,
    )


def shards(
    tokens,
    out_grad,
    logit_grad,
    piece_start,
    piece_len,
    qkv_weight,
    query_bias,
    value_bias,
    out_weight,
    out_bias,
    gain_one,
    shift_one,
    in_weight,
    in_bias,
    back_weight,
    back_bias,
    gain_two,
    shift_two,
    reduce_weight,
    reduce_bias,
    pool_query,
    pool_weight,
    pool_bias,
    class_weight,
    class_bias,
):
    seq_count, local_len, width = tokens.shape
    hidden_units = in_weight.shape[1]
    full_len = local_len * lax.axis_size("ctx")
    head_width = RED // PH
    query_pos = lax.axis_index("ctx") * local_len + jnp.arange(local_len, dtype=jnp.int32)
    key_pos = jnp.arange(full_len, dtype=jnp.int32)
    lead_mask = (lax.axis_index("ctx") == 0).astype(jnp.float32)
    query_rows = pool_query.astype(jnp.float32).reshape(PH, head_width)
    pool_weight_f = pool_weight.astype(jnp.float32)
    class_weight_f = class_weight.astype(jnp.float32)
    reduce_shift = reduce_bias.astype(jnp.float32)
    pool_shift = pool_bias.astype(jnp.float32)
    class_shift = class_bias.astype(jnp.float32)

    def one_sequence(totals, inputs):
        seq_tokens, seq_out_grad, seq_logit, seq_starts, seq_lengths = inputs
        starts = seq_starts[None]
        lengths = seq_lengths[None]
        logit_row = seq_logit[None]
        gathered = (
            lax.all_gather(qkv_weight, ("dp", "ctx"), axis=0, tiled=True),
            lax.all_gather(out_weight, ("dp", "ctx"), axis=0, tiled=True),
            lax.all_gather(in_weight, ("dp", "ctx"), axis=0, tiled=True),
            lax.all_gather(back_weight, ("dp", "ctx"), axis=0, tiled=True),
            lax.all_gather(reduce_weight, ("dp", "ctx"), axis=0, tiled=True),
            lax.all_gather(query_bias, ("dp", "ctx"), axis=0, tiled=True),
            lax.all_gather(value_bias, ("dp", "ctx"), axis=0, tiled=True),
            lax.all_gather(out_bias, ("dp", "ctx"), axis=0, tiled=True),
            lax.all_gather(gain_one, ("dp", "ctx"), axis=0, tiled=True),
            lax.all_gather(shift_one, ("dp", "ctx"), axis=0, tiled=True),
            lax.all_gather(in_bias, ("dp", "ctx"), axis=0, tiled=True),
            lax.all_gather(back_bias, ("dp", "ctx"), axis=0, tiled=True),
            lax.all_gather(gain_two, ("dp", "ctx"), axis=0, tiled=True),
            lax.all_gather(shift_two, ("dp", "ctx"), axis=0, tiled=True),
        )
        qkv_full, out_full, in_full, back_full, reduce_full = gathered[:5]
        q_bias, v_bias, o_bias, g_one, s_one, i_bias, b_bias, g_two, s_two = [
            member.astype(jnp.float32) for member in gathered[5:]
        ]
        qkv_shift = jnp.concatenate([q_bias, jnp.zeros_like(q_bias), v_bias])
        qkv_low = (
            jnp.dot(seq_tokens, qkv_full, preferred_element_type=jnp.float32) + qkv_shift
        ).astype(jnp.bfloat16)
        queries = qkv_low[:, :width].reshape(1, local_len, H, HD)
        keys_local = qkv_low[:, width : 2 * width].reshape(1, local_len, width)
        values_local = qkv_low[:, 2 * width :].reshape(1, local_len, width)
        keys_all, values_all = (
            lax.all_gather(keys_local, "ctx", axis=1, tiled=True),
            lax.all_gather(values_local, "ctx", axis=1, tiled=True),
        )
        key_blocks = keys_all.reshape(1, full_len, H, HD)
        value_blocks = values_all.reshape(1, full_len, H, HD)
        mixed_block, log_total = attend_block(
            query_pos, key_pos, (queries, key_blocks, value_blocks, starts, lengths)
        )
        mixed_low = mixed_block.reshape(local_len, width)
        attended = jnp.dot(mixed_low, out_full, preferred_element_type=jnp.float32) + o_bias
        first_norm, normed_one, inv_one = norm_rows(
            seq_tokens.astype(jnp.float32) + attended, g_one, s_one
        )
        first_low = first_norm.astype(jnp.bfloat16)
        inner_pre = jnp.dot(first_low, in_full, preferred_element_type=jnp.float32) + i_bias
        active, gelu_back = jax.vjp(partial(jax.nn.gelu, approximate=False), inner_pre)
        active_low = active.astype(jnp.bfloat16)
        branch = jnp.dot(active_low, back_full, preferred_element_type=jnp.float32) + b_bias
        result, normed_two, inv_two = norm_rows(first_norm + branch, g_two, s_two)
        result_low = result.astype(jnp.bfloat16)
        reduced = (
            jnp.dot(result_low, reduce_full, preferred_element_type=jnp.float32) + reduce_shift
        )
        pool_heads = reduced.reshape(1, local_len, PH, head_width)
        pool_scores = jnp.einsum("blpe,pe->blp", pool_heads, query_rows, precision=highest) * 0.125
        local_top = jnp.max(pool_scores, axis=1)
        pool_exp = jnp.exp(pool_scores - local_top[:, None])
        local_sum = jnp.einsum("blp,blpe->bpe", pool_exp, pool_heads, precision=highest).reshape(
            1, RED
        )
        pool_top, pool_total, pool_sum = joined(
            (local_top, jnp.sum(pool_exp, axis=1), local_sum), "ctx", join_stats
        )
        pooled_heads = pool_sum.reshape(1, PH, head_width) / pool_total[:, :, None]
        pooled = pooled_heads.reshape(1, RED)
        hidden = jnp.tanh(jnp.dot(pooled, pool_weight_f, precision=highest) + pool_shift)
        logits = jnp.dot(hidden, class_weight_f, precision=highest) + class_shift
        back_set = (
            lax.all_gather(qkv_weight, ("dp", "ctx"), axis=0, tiled=True),
            lax.all_gather(out_weight, ("dp", "ctx"), axis=0, tiled=True),
            lax.all_gather(in_weight, ("dp", "ctx"), axis=0, tiled=True),
            lax.all_gather(back_weight, ("dp", "ctx"), axis=0, tiled=True),
            lax.all_gather(reduce_weight, ("dp", "ctx"), axis=0, tiled=True),
            lax.all_gather(gain_one, ("dp", "ctx"), axis=0, tiled=True),
            lax.all_gather(gain_two, ("dp", "ctx"), axis=0, tiled=True),
        )
        qkv_back, out_back, in_back, back_back, reduce_back = back_set[:5]
        gain_back_one = back_set[5].astype(jnp.float32)
        gain_back_two = back_set[6].astype(jnp.float32)
        grad_class = rows_product(hidden, logit_row, highest) * lead_mask
        grad_class_bias = jnp.sum(logit_row, axis=0) * lead_mask
        grad_hidden = right_transposed(logit_row, class_weight_f, highest)
        grad_pre = grad_hidden * (1.0 - hidden * hidden)
        grad_pool_weight = rows_product(pooled, grad_pre, highest) * lead_mask
        grad_pool_bias = jnp.sum(grad_pre, axis=0) * lead_mask
        grad_pooled = right_transposed(grad_pre, pool_weight_f, highest).reshape(1, PH, head_width)
        pool_probs = jnp.exp(pool_scores - (pool_top + jnp.log(pool_total))[:, None])
        pool_along = (
            jnp.einsum("blpe,bpe->blp", pool_heads, grad_pooled, precision=highest)
            - jnp.sum(pooled_heads * grad_pooled, axis=-1)[:, None]
        )
        grad_pool_scores = pool_probs * pool_along
        grad_reduced = (
            pool_probs[..., None] * grad_pooled[:, None]
            + grad_pool_scores[..., None] * query_rows * 0.125
        )
        grad_query = (
            jnp.einsum("blp,blpe->pe", grad_pool_scores, pool_heads, precision=highest).reshape(RED)
            * 0.125
        )
        grad_red_low = grad_reduced.reshape(local_len, RED).astype(jnp.bfloat16)
        grad_reduce_bias = jnp.sum(grad_red_low.astype(jnp.float32), axis=0)
        grad_reduce = rows_product(result_low, grad_red_low)
        grad_result = seq_out_grad.astype(jnp.float32) + right_transposed(grad_red_low, reduce_back)
        grad_gain_two = jnp.sum(grad_result * normed_two, axis=0)
        grad_shift_two = jnp.sum(grad_result, axis=0)
        grad_mid = norm_back(grad_result, normed_two, inv_two, gain_back_two)
        grad_branch_low = grad_mid.astype(jnp.bfloat16)
        grad_back_bias = jnp.sum(grad_branch_low.astype(jnp.float32), axis=0)
        grad_back = rows_product(active_low, grad_branch_low)
        grad_active = right_transposed(grad_branch_low, back_back)
        grad_inner_low = gelu_back(grad_active)[0].astype(jnp.bfloat16)
        grad_in_bias = jnp.sum(grad_inner_low.astype(jnp.float32), axis=0)
        grad_in = rows_product(first_low, grad_inner_low)
        grad_first = grad_mid + right_transposed(grad_inner_low, in_back)
        grad_gain_one = jnp.sum(grad_first * normed_one, axis=0)
        grad_shift_one = jnp.sum(grad_first, axis=0)
        grad_start = norm_back(grad_first, normed_one, inv_one, gain_back_one)
        grad_attn_low = grad_start.astype(jnp.bfloat16)
        grad_out_bias = jnp.sum(grad_attn_low.astype(jnp.float32), axis=0)
        grad_out = rows_product(mixed_low, grad_attn_low)
        grad_mixed_low = (
            right_transposed(grad_attn_low, out_back)
            .astype(jnp.bfloat16)
            .reshape(1, local_len, H, HD)
        )
        keys_back, values_back = (
            lax.all_gather(keys_local, "ctx", axis=1, tiled=True),
            lax.all_gather(values_local, "ctx", axis=1, tiled=True),
        )
        keys_back = keys_back.reshape(1, full_len, H, HD)
        values_back = values_back.reshape(1, full_len, H, HD)
        grad_queries, grad_keys, grad_values = attend_back(
            query_pos,
            key_pos,
            (queries, keys_back, values_back, starts, lengths, log_total, grad_mixed_low),
        )
        grad_keys_own, grad_values_own = (
            lax.psum_scatter(
                grad_keys.reshape(1, full_len, width).astype(jnp.bfloat16),
                "ctx",
                scatter_dimension=1,
                tiled=True,
            ).astype(jnp.float32),
            lax.psum_scatter(
                grad_values.reshape(1, full_len, width).astype(jnp.bfloat16),
                "ctx",
                scatter_dimension=1,
                tiled=True,
            ).astype(jnp.float32),
        )
        grad_qkv_low = jnp.concatenate(
            [
                grad_queries.reshape(local_len, width),
                grad_keys_own.reshape(local_len, width),
                grad_values_own.reshape(local_len, width),
            ],
            axis=1,
        ).astype(jnp.bfloat16)
        grad_qkv_float = grad_qkv_low.astype(jnp.float32)
        grad_query_bias = jnp.sum(grad_qkv_float[:, :width], axis=0)
        grad_value_bias = jnp.sum(grad_qkv_float[:, 2 * width :], axis=0)
        grad_qkv = rows_product(seq_tokens, grad_qkv_low)
        token_grad = (grad_start + right_transposed(grad_qkv_low, qkv_back)).astype(jnp.bfloat16)
        terms = (
            grad_qkv,
            grad_query_bias,
            grad_value_bias,
            grad_out,
            grad_out_bias,
            grad_gain_one,
            grad_shift_one,
            grad_in,
            grad_in_bias,
            grad_back,
            grad_back_bias,
            grad_gain_two,
            grad_shift_two,
            grad_reduce,
            grad_reduce_bias,
            grad_query,
            grad_pool_weight,
            grad_pool_bias,
            grad_class,
            grad_class_bias,
        )
        updated = tuple((total + term for total, term in zip(totals, terms)))
        return (updated, (result_low, logits[0], token_grad))

    vector_d = jnp.zeros((width,), jnp.float32)
    vector_red = jnp.zeros((RED,), jnp.float32)
    zeros = (
        jnp.zeros((width, 3 * width), jnp.float32),
        vector_d,
        vector_d,
        jnp.zeros((width, width), jnp.float32),
        vector_d,
        vector_d,
        vector_d,
        jnp.zeros((width, hidden_units), jnp.float32),
        jnp.zeros((hidden_units,), jnp.float32),
        jnp.zeros((hidden_units, width), jnp.float32),
        vector_d,
        vector_d,
        vector_d,
        jnp.zeros((width, RED), jnp.float32),
        vector_red,
        vector_red,
        jnp.zeros((RED, RED), jnp.float32),
        vector_red,
        jnp.zeros((RED, CLS), jnp.float32),
        jnp.zeros((CLS,), jnp.float32),
    )
    totals, stacked = lax.scan(
        one_sequence, zeros, (tokens, out_grad, logit_grad, piece_start, piece_len)
    )
    layer_out, logits, token_grad = stacked
    owned = (
        lax.psum_scatter(totals[0], ("dp", "ctx"), scatter_dimension=0, tiled=True),
        lax.psum_scatter(totals[1], ("dp", "ctx"), scatter_dimension=0, tiled=True),
        lax.psum_scatter(totals[2], ("dp", "ctx"), scatter_dimension=0, tiled=True),
        lax.psum_scatter(totals[3], ("dp", "ctx"), scatter_dimension=0, tiled=True),
        lax.psum_scatter(totals[4], ("dp", "ctx"), scatter_dimension=0, tiled=True),
        lax.psum_scatter(totals[5], ("dp", "ctx"), scatter_dimension=0, tiled=True),
        lax.psum_scatter(totals[6], ("dp", "ctx"), scatter_dimension=0, tiled=True),
        lax.psum_scatter(totals[7], ("dp", "ctx"), scatter_dimension=0, tiled=True),
        lax.psum_scatter(totals[8], ("dp", "ctx"), scatter_dimension=0, tiled=True),
        lax.psum_scatter(totals[9], ("dp", "ctx"), scatter_dimension=0, tiled=True),
        lax.psum_scatter(totals[10], ("dp", "ctx"), scatter_dimension=0, tiled=True),
        lax.psum_scatter(totals[11], ("dp", "ctx"), scatter_dimension=0, tiled=True),
        lax.psum_scatter(totals[12], ("dp", "ctx"), scatter_dimension=0, tiled=True),
        lax.psum_scatter(totals[13], ("dp", "ctx"), scatter_dimension=0, tiled=True),
    )
    summed = lax.psum(
        (totals[14], totals[15], totals[16], totals[17], totals[18], totals[19]), ("dp", "ctx")
    )
    return (
        layer_out,
        logits,
        token_grad,
        owned[0],
        owned[1],
        owned[2],
        owned[3],
        owned[4],
        owned[5],
        owned[6],
        owned[7],
        owned[8],
        owned[9],
        owned[10],
        owned[11],
        owned[12],
        owned[13],
        summed[0],
        summed[1],
        summed[2],
        summed[3],
        summed[4],
        summed[5],
    )


def solution(mesh):
    placed = (
        P("dp", "ctx", None),
        P("dp", "ctx", None),
        P("dp", None),
        P("dp", None),
        P("dp", None),
        P(("dp", "ctx"), None),
        P(("dp", "ctx")),
        P(("dp", "ctx")),
        P(("dp", "ctx"), None),
        P(("dp", "ctx")),
        P(("dp", "ctx")),
        P(("dp", "ctx")),
        P(("dp", "ctx"), None),
        P(("dp", "ctx")),
        P(("dp", "ctx"), None),
        P(("dp", "ctx")),
        P(("dp", "ctx")),
        P(("dp", "ctx")),
        P(("dp", "ctx"), None),
        P(),
        P(),
        P(),
        P(),
        P(),
        P(),
    )
    return jax.shard_map(
        shards,
        mesh=mesh,
        in_specs=placed,
        out_specs=(
            P("dp", "ctx", None),
            P("dp", None),
            P("dp", "ctx", None),
            P(("dp", "ctx"), None),
            P(("dp", "ctx")),
            P(("dp", "ctx")),
            P(("dp", "ctx"), None),
            P(("dp", "ctx")),
            P(("dp", "ctx")),
            P(("dp", "ctx")),
            P(("dp", "ctx"), None),
            P(("dp", "ctx")),
            P(("dp", "ctx"), None),
            P(("dp", "ctx")),
            P(("dp", "ctx")),
            P(("dp", "ctx")),
            P(("dp", "ctx"), None),
            P(),
            P(),
            P(),
            P(),
            P(),
            P(),
        ),
        check_vma=False,
    )
```

profile of v0, /device:TPU:0, one launch (start us, length us, event | category | flops | bytes accessed | tf_op | source)
XLA Modules:
  0.0 1833.4 jit_solution(3636473105227695090)
XLA Ops:
  15.6 1069.9 %while.66 = (s32[]{:T(128)}, f32[768,2304]{1,0:T(8,128)}, f32[768]{0:T(1024)}, f32[768]{0:T(1024)}, f32[768,768]{1,0:T(8,128)}, /*index=5*/f32[768]{0:T(1024)}, ...) while((s32[]{:T(128)}, f32[768,2304]{1,0:T(8,128)}, ...), condition=%wide.region_29.30_spmd.clone.clone, body=%wide.region_0.29_spmd.clone.clone.sunk | while | flops 27319658496 | bytes 705549568 | solution.py:405
  24.0 42.5 %all-reduce.37 = (bf16[768]{0:T(1024)(128)(2,1)S(1)}, bf16[768]{0:T(1024)(128)(2,1)S(1)}, bf16[768]{0:T(1024)(128)(2,1)S(1)}, bf16[768]{0:T(1024)(128)(2,1)S(1)}...) all-reduce(bf16[768]{0:T(1024)(128)(2,1)S(1)} %dynamic-update-slice, ...), channel_id=1, replica_groups=mesh['dp'=16,'ctx'=2] {'dp','ctx'}, use_global_device_ids=true, to_apply=%add.1 | all-reduce | flops 9216 | bytes 36864 | tf_op jit(solution)/shard_map/while
  66.5 15.6 all-gather.19.cloned.1.call-done
  91.3 73.5 %all_gather.193 = bf16[768,128]{1,0:T(8,128)(2,1)} all-gather(bf16[24,128]{1,0:T(8,128)(2,1)S(1)} %copy-done.47), channel_id=1, replica_groups=mesh['dp'=16,'ctx'=2] {'dp','ctx'}, dimensions={0}, use_global_device_ids=true | all-gather | bytes 202752 | tf_op jit(solution)/shard_map/while/body/eval_jaxpr/all_gather | solution.py:199
  180.8 12.3 exponential_reduce_fusion.2
  193.2 11.2 convolution_convert_fusion.6
  207.4 59.5 %all-gather.25.cloned.1.call-done = bf16[768,3072]{1,0:T(8,128)(2,1)} async-done(((bf16[24,3072]{1,0:T(8,128)(2,1)}), bf16[768,3072]{1,0:T(8,128)(2,1)}) %all-gather.25.cloned.1.call-update) | async-done | bytes 4718608 | tf_op jit(solution)/shard_map/while/body/eval_jaxpr/all_gather | solution.py:197
  266.9 19.8 %multiply_convert_fusion.3 = (bf16[512,3072]{1,0:T(8,128)(2,1)}, f32[512,3072]{1,0:T(8,128)}, f32[512,3072]{1,0:T(8,128)}) fusion(f32[3072]{0:T(1024)S(1)} %convert_element_type.519, bf16[768,3072]{1,0:T(8,128)(2,1)} %all-gather.25.cloned.1.call-done, f32[512,768]{1,0:T(8,128)S(1)} %get-tuple-element.1699, f32[768]{0:T(1024)S(1)} %convert_element_type.520, ...), kind=kOutput, calls=%fused_computation.20.clone.1 | convolution fusion | flops 2521694208 | bytes 22042624 | tf_op jit(solution)/shard_map/while/body/eval_jaxpr/dot_general | solution.py:236
  286.7 44.9 %all-gather.27.cloned.1.call-done = bf16[3072,768]{1,0:T(8,128)(2,1)} async-done(((bf16[96,768]{1,0:T(8,128)(2,1)}), bf16[3072,768]{1,0:T(8,128)(2,1)}) %all-gather.27.cloned.1.call-update) | async-done | bytes 4718608 | tf_op jit(solution)/shard_map/while/body/eval_jaxpr/all_gather | solution.py:198
  380.0 13.2 convolution_convert_fusion.8
  398.5 12.0 fusion.319
  410.8 54.1 %fusion.320 = bf16[12,64,1024]{2,1,0:T(8,128)(2,1)} fusion(bf16[512,12,64]{0,2,1:T(8,128)(2,1)} %bitcast.462, f32[12,512,1024]{2,1,0:T(8,128)} %fusion.319, f32[12,512]{1,0:T(8,128)} %copy-done.30, f32[12,512,1024]{2,1,0:T(8,128)} %get-tuple-element.1698, pred[512,1024]{1,0:T(8,128)(4,1)} %copy-done.10), kind=kOutput, calls=%fused_computation.40.clone.1 | convolution fusion | flops 875305984 | bytes 53239808 | tf_op jit(solution)/shard_map/while/body/eval_jaxpr/ghqk,gqhe->gkhe/dot_general | solution.py:122
  467.4 53.8 %fusion.321 = bf16[12,64,512]{2,1,0:T(8,128)(2,1)} fusion(bf16[1024,12,64]{0,2,1:T(8,128)(2,1)} %bitcast.451, f32[12,512,1024]{2,1,0:T(8,128)} %fusion.319, f32[12,512]{1,0:T(8,128)} %copy-done.30, f32[12,512,1024]{2,1,0:T(8,128)} %get-tuple-element.1698, pred[512,1024]{1,0:T(8,128)(4,1)} %copy-done.10), kind=kOutput, calls=%fused_computation.63.clone.1 | convolution fusion | flops 874912768 | bytes 53239808 | tf_op jit(solution)/shard_map/while/body/eval_jaxpr/ghqk,gkhe->gqhe/dot_general | solution.py:119
  555.4 40.1 %all-reduce.37 = (bf16[768]{0:T(1024)(128)(2,1)S(1)}, bf16[768]{0:T(1024)(128)(2,1)S(1)}, bf16[768]{0:T(1024)(128)(2,1)S(1)}, bf16[768]{0:T(1024)(128)(2,1)S(1)}...) all-reduce(bf16[768]{0:T(1024)(128)(2,1)S(1)} %dynamic-update-slice, ...), channel_id=1, replica_groups=mesh['dp'=16,'ctx'=2] {'dp','ctx'}, use_global_device_ids=true, to_apply=%add.1 | all-reduce | flops 9216 | bytes 36864 | tf_op jit(solution)/shard_map/while
  595.5 13.8 all-gather.19.cloned.1.call-done
  618.7 73.5 %all_gather.193 = bf16[768,128]{1,0:T(8,128)(2,1)} all-gather(bf16[24,128]{1,0:T(8,128)(2,1)S(1)} %copy-done.47), channel_id=1, replica_groups=mesh['dp'=16,'ctx'=2] {'dp','ctx'}, dimensions={0}, use_global_device_ids=true | all-gather | bytes 202752 | tf_op jit(solution)/shard_map/while/body/eval_jaxpr/all_gather | solution.py:199
  708.1 12.3 exponential_reduce_fusion.2
  720.5 11.2 convolution_convert_fusion.6
  734.8 59.7 %all-gather.25.cloned.1.call-done = bf16[768,3072]{1,0:T(8,128)(2,1)} async-done(((bf16[24,3072]{1,0:T(8,128)(2,1)}), bf16[768,3072]{1,0:T(8,128)(2,1)}) %all-gather.25.cloned.1.call-update) | async-done | bytes 4718608 | tf_op jit(solution)/shard_map/while/body/eval_jaxpr/all_gather | solution.py:197
  794.4 19.8 %multiply_convert_fusion.3 = (bf16[512,3072]{1,0:T(8,128)(2,1)}, f32[512,3072]{1,0:T(8,128)}, f32[512,3072]{1,0:T(8,128)}) fusion(f32[3072]{0:T(1024)S(1)} %convert_element_type.519, bf16[768,3072]{1,0:T(8,128)(2,1)} %all-gather.25.cloned.1.call-done, f32[512,768]{1,0:T(8,128)S(1)} %get-tuple-element.1699, f32[768]{0:T(1024)S(1)} %convert_element_type.520, ...), kind=kOutput, calls=%fused_computation.20.clone.1 | convolution fusion | flops 2521694208 | bytes 22042624 | tf_op jit(solution)/shard_map/while/body/eval_jaxpr/dot_general | solution.py:236
  814.2 44.9 %all-gather.27.cloned.1.call-done = bf16[3072,768]{1,0:T(8,128)(2,1)} async-done(((bf16[96,768]{1,0:T(8,128)(2,1)}), bf16[3072,768]{1,0:T(8,128)(2,1)}) %all-gather.27.cloned.1.call-update) | async-done | bytes 4718608 | tf_op jit(solution)/shard_map/while/body/eval_jaxpr/all_gather | solution.py:198
  907.6 13.2 convolution_convert_fusion.8
  926.1 12.0 fusion.319
  938.3 54.1 %fusion.320 = bf16[12,64,1024]{2,1,0:T(8,128)(2,1)} fusion(bf16[512,12,64]{0,2,1:T(8,128)(2,1)} %bitcast.462, f32[12,512,1024]{2,1,0:T(8,128)} %fusion.319, f32[12,512]{1,0:T(8,128)} %copy-done.30, f32[12,512,1024]{2,1,0:T(8,128)} %get-tuple-element.1698, pred[512,1024]{1,0:T(8,128)(4,1)} %copy-done.10), kind=kOutput, calls=%fused_computation.40.clone.1 | convolution fusion | flops 875305984 | bytes 53239808 | tf_op jit(solution)/shard_map/while/body/eval_jaxpr/ghqk,gqhe->gkhe/dot_general | solution.py:122
  995.0 53.8 %fusion.321 = bf16[12,64,512]{2,1,0:T(8,128)(2,1)} fusion(bf16[1024,12,64]{0,2,1:T(8,128)(2,1)} %bitcast.451, f32[12,512,1024]{2,1,0:T(8,128)} %fusion.319, f32[12,512]{1,0:T(8,128)} %copy-done.30, f32[12,512,1024]{2,1,0:T(8,128)} %get-tuple-element.1698, pred[512,1024]{1,0:T(8,128)(4,1)} %copy-done.10), kind=kOutput, calls=%fused_computation.63.clone.1 | convolution fusion | flops 874912768 | bytes 53239808 | tf_op jit(solution)/shard_map/while/body/eval_jaxpr/ghqk,gkhe->gqhe/dot_general | solution.py:119
  1089.6 40.5 %all-reduce.34 = (f32[768]{0:T(1024)S(1)}, f32[768]{0:T(1024)S(1)}, f32[768]{0:T(1024)S(1)}, f32[768]{0:T(1024)S(1)}, f32[768]{0:T(1024)S(1)}, /*index=5*/f32[30...) all-reduce(f32[768]{0:T(1024)S(1)} %copy-done.71, ...), channel_id=9, replica_groups=mesh['dp'=16,'ctx'=2] {'dp','ctx'}, use_global_device_ids=true, to_apply=%region_31.32.clone | all-reduce | flops 11406 | bytes 91248
  1135.4 74.3 %all-reduce.41.cloned.1.call-done = f32[128,128]{1,0:T(8,128)} async-done(((f32[128,128]{1,0:T(8,128)}), f32[128,128]{1,0:T(8,128)}) %all-reduce.41.cloned.1.call-update) | async-done | bytes 65552 | tf_op jit(solution)/shard_map/psum | solution.py:425
  1209.7 102.1 %reduce-scatter.18.cloned.1.call-done = f32[24,128]{1,0:T(8,128)} async-done(((f32[768,128]{1,0:T(8,128)}), f32[24,128]{1,0:T(8,128)}) %reduce-scatter.18.cloned.1.call-update) | async-done | bytes 12304
  1311.8 104.5 %reduce-scatter.12.cloned.1.call-done = f32[24,768]{1,0:T(8,128)} async-done(((f32[768,768]{1,0:T(8,128)}), f32[24,768]{1,0:T(8,128)}) %reduce-scatter.12.cloned.1.call-update) | async-done | bytes 73744 | tf_op jit(solution)/shard_map/reduce_scatter | solution.py:413
  1416.3 124.8 %reduce-scatter.10.cloned.1.call-done = f32[24,2304]{1,0:T(8,128)} async-done(((f32[768,2304]{1,0:T(8,128)}), f32[24,2304]{1,0:T(8,128)}) %reduce-scatter.10.cloned.1.call-update) | async-done | bytes 221200 | tf_op jit(solution)/shard_map/reduce_scatter | solution.py:410
  1541.1 141.8 %reduce-scatter.14.cloned.1.call-done = f32[24,3072]{1,0:T(8,128)} async-done(((f32[768,3072]{1,0:T(8,128)}), f32[24,3072]{1,0:T(8,128)}) %reduce-scatter.14.cloned.1.call-update) | async-done | bytes 294928 | tf_op jit(solution)/shard_map/reduce_scatter | solution.py:417
  1682.8 141.7 %reduce-scatter.16.cloned.1.call-done = f32[96,768]{1,0:T(8,128)} async-done(((f32[3072,768]{1,0:T(8,128)}), f32[96,768]{1,0:T(8,128)}) %reduce-scatter.16.cloned.1.call-update) | async-done | bytes 294928 | tf_op jit(solution)/shard_map/reduce_scatter | solution.py:419
  (824 shorter events, 259.9 us)
Async XLA Ops:
  15.6 337.8 %copy-start.28 = (f32[128,14]{0,1:T(8,128)}, f32[128,14]{0,1:T(8,128)S(1)}, u32[]{:S(2)}) copy-start(f32[128,14]{0,1:T(8,128)S(1)} %get-tuple-element.1922) | copy-start | bytes 21508 | tf_op jit(solution)/shard_map/while
  15.6 338.0 %copy-start.24 = (f32[128,128]{1,0:T(8,128)}, f32[128,128]{1,0:T(8,128)S(1)}, u32[]{:S(2)}) copy-start(f32[128,128]{1,0:T(8,128)S(1)} %get-tuple-element.1923) | copy-start | bytes 196612 | tf_op jit(solution)/shard_map/while
  15.6 66.5 %all-gather.19.cloned.1.call-start = ((), (), s32[]{:S(2)}) async-start(), calls=%async_computation.14 | async-start | bytes 3649536 | tf_op jit(solution)/shard_map/while/body/eval_jaxpr/all_gather | solution.py:195
  16.3 150.1 %all-gather.23.cloned.1.call-start = ((), (), s32[]{:S(2)}) async-start(), calls=%async_computation.16 | async-start | bytes 2359296 | tf_op jit(solution)/shard_map/while/body/eval_jaxpr/all_gather | solution.py:319
  87.8 91.3 %all-gather.21.cloned.1.call-start = ((), (), s32[]{:S(2)}) async-start(), calls=%async_computation.15 | async-start | bytes 2359296 | tf_op jit(solution)/shard_map/while/body/eval_jaxpr/all_gather | solution.py:223
  88.5 115.9 %all-gather.17.cloned.1.call-start = ((), (), s32[]{:S(2)}) async-start(), calls=%async_computation.13 | async-start | bytes 1216512 | tf_op jit(solution)/shard_map/while/body/eval_jaxpr/all_gather | solution.py:196
  89.1 177.8 %all-gather.25.cloned.1.call-start = ((), (), s32[]{:S(2)}) async-start(), calls=%async_computation.17 | async-start | bytes 4866048 | tf_op jit(solution)/shard_map/while/body/eval_jaxpr/all_gather | solution.py:197
  89.7 241.8 %all-gather.27.cloned.1.call-start = ((), (), s32[]{:S(2)}) async-start(), calls=%async_computation.18 | async-start | bytes 4866048 | tf_op jit(solution)/shard_map/while/body/eval_jaxpr/all_gather | solution.py:198
  90.3 445.4 %reduce-scatter.20.cloned.1.call-start = ((), (), s32[]{:S(2)}) async-start(), calls=%async_computation.19 | async-start | bytes 2359296 | tf_op jit(solution)/shard_map/while/body/eval_jaxpr/reduce_scatter | solution.py:336
  91.2 175.7 %copy-start.37 = (f32[3072]{0:T(1024)}, f32[3072]{0:T(1024)S(1)}, u32[]{:S(2)}) copy-start(f32[3072]{0:T(1024)S(1)} %convert_element_type.519) | copy-start | bytes 36868 | tf_op jit(solution)/shard_map/while
  204.4 82.3 %copy-start.17 = (bf16[12,64,512]{2,1,0:T(8,128)(2,1)}, bf16[12,64,512]{2,1,0:T(8,128)(2,1)S(1)}, u32[]{:S(2)}) copy-start(bf16[12,64,512]{2,1,0:T(8,128)(2,1)S(1)} %convolution_convert_fusion.6) | copy-start | bytes 2359300 | tf_op jit(solution)/shard_map/while
  393.2 142.4 %reduce-scatter.22.cloned.1.call-start = ((), (), s32[]{:S(2)}) async-start(), calls=%async_computation.20 | async-start | bytes 2359296 | tf_op jit(solution)/shard_map/while/body/eval_jaxpr/reduce_scatter | solution.py:330
  410.7 56.2 %copy-start.4 = (bf16[512,768]{1,0:T(8,128)(2,1)S(1)}, bf16[512,768]{1,0:T(8,128)(2,1)}, u32[]{:S(2)}) copy-start(bf16[512,768]{1,0:T(8,128)(2,1)} %copy-done.3) | copy-start | bytes 2359300 | tf_op jit(solution)/shard_map/while
  547.1 333.9 %copy-start.28 = (f32[128,14]{0,1:T(8,128)}, f32[128,14]{0,1:T(8,128)S(1)}, u32[]{:S(2)}) copy-start(f32[128,14]{0,1:T(8,128)S(1)} %get-tuple-element.1922) | copy-start | bytes 21508 | tf_op jit(solution)/shard_map/while
  547.1 334.0 %copy-start.24 = (f32[128,128]{1,0:T(8,128)}, f32[128,128]{1,0:T(8,128)S(1)}, u32[]{:S(2)}) copy-start(f32[128,128]{1,0:T(8,128)S(1)} %get-tuple-element.1923) | copy-start | bytes 196612 | tf_op jit(solution)/shard_map/while
  547.1 62.3 %all-gather.19.cloned.1.call-start = ((), (), s32[]{:S(2)}) async-start(), calls=%async_computation.14 | async-start | bytes 3649536 | tf_op jit(solution)/shard_map/while/body/eval_jaxpr/all_gather | solution.py:195
  547.8 145.9 %all-gather.23.cloned.1.call-start = ((), (), s32[]{:S(2)}) async-start(), calls=%async_computation.16 | async-start | bytes 2359296 | tf_op jit(solution)/shard_map/while/body/eval_jaxpr/all_gather | solution.py:319
  615.0 91.3 %all-gather.21.cloned.1.call-start = ((), (), s32[]{:S(2)}) async-start(), calls=%async_computation.15 | async-start | bytes 2359296 | tf_op jit(solution)/shard_map/while/body/eval_jaxpr/all_gather | solution.py:223
  615.8 116.0 %all-gather.17.cloned.1.call-start = ((), (), s32[]{:S(2)}) async-start(), calls=%async_computation.13 | async-start | bytes 1216512 | tf_op jit(solution)/shard_map/while/body/eval_jaxpr/all_gather | solution.py:196
  616.3 178.1 %all-gather.25.cloned.1.call-start = ((), (), s32[]{:S(2)}) async-start(), calls=%async_computation.17 | async-start | bytes 4866048 | tf_op jit(solution)/shard_map/while/body/eval_jaxpr/all_gather | solution.py:197
  617.1 242.0 %all-gather.27.cloned.1.call-start = ((), (), s32[]{:S(2)}) async-start(), calls=%async_computation.18 | async-start | bytes 4866048 | tf_op jit(solution)/shard_map/while/body/eval_jaxpr/all_gather | solution.py:198
  617.7 451.0 %reduce-scatter.20.cloned.1.call-start = ((), (), s32[]{:S(2)}) async-start(), calls=%async_computation.19 | async-start | bytes 2359296 | tf_op jit(solution)/shard_map/while/body/eval_jaxpr/reduce_scatter | solution.py:336
  618.6 175.8 %copy-start.37 = (f32[3072]{0:T(1024)}, f32[3072]{0:T(1024)S(1)}, u32[]{:S(2)}) copy-start(f32[3072]{0:T(1024)S(1)} %convert_element_type.519) | copy-start | bytes 36868 | tf_op jit(solution)/shard_map/while
  731.7 82.5 %copy-start.17 = (bf16[12,64,512]{2,1,0:T(8,128)(2,1)}, bf16[12,64,512]{2,1,0:T(8,128)(2,1)S(1)}, u32[]{:S(2)}) copy-start(bf16[12,64,512]{2,1,0:T(8,128)(2,1)S(1)} %convolution_convert_fusion.6) | copy-start | bytes 2359300 | tf_op jit(solution)/shard_map/while
  920.8 148.0 %reduce-scatter.22.cloned.1.call-start = ((), (), s32[]{:S(2)}) async-start(), calls=%async_computation.20 | async-start | bytes 2359296 | tf_op jit(solution)/shard_map/while/body/eval_jaxpr/reduce_scatter | solution.py:330
  938.3 56.2 %copy-start.4 = (bf16[512,768]{1,0:T(8,128)(2,1)S(1)}, bf16[512,768]{1,0:T(8,128)(2,1)}, u32[]{:S(2)}) copy-start(bf16[512,768]{1,0:T(8,128)(2,1)} %copy-done.3) | copy-start | bytes 2359300 | tf_op jit(solution)/shard_map/while
  1085.5 124.2 %all-reduce.41.cloned.1.call-start = ((), (), s32[]{:S(2)}) async-start(), calls=%async_computation.11 | async-start | bytes 131072 | tf_op jit(solution)/shard_map/psum | solution.py:425
  1086.1 225.7 %reduce-scatter.18.cloned.1.call-start = ((), (), s32[]{:S(2)}) async-start(), calls=%async_computation.12 | async-start | bytes 405504
  1086.7 329.6 %reduce-scatter.12.cloned.1.call-start = ((), (), s32[]{:S(2)}) async-start(), calls=%async_computation.8 | async-start | bytes 2433024 | tf_op jit(solution)/shard_map/reduce_scatter | solution.py:413
  1087.3 453.8 %reduce-scatter.10.cloned.1.call-start = ((), (), s32[]{:S(2)}) async-start(), calls=%async_computation.7 | async-start | bytes 7299072 | tf_op jit(solution)/shard_map/reduce_scatter | solution.py:410
  1088.0 594.9 %reduce-scatter.14.cloned.1.call-start = ((), (), s32[]{:S(2)}) async-start(), calls=%async_computation.9 | async-start | bytes 9732096 | tf_op jit(solution)/shard_map/reduce_scatter | solution.py:417
  1088.8 735.8 %reduce-scatter.16.cloned.1.call-start = ((), (), s32[]{:S(2)}) async-start(), calls=%async_computation.10 | async-start | bytes 9732096 | tf_op jit(solution)/shard_map/reduce_scatter | solution.py:419
  (222 other events, 4194.6 us)
Sparse Core Ops, SparseCore 0:
  19.3 62.7 all-gather.18
  87.9 27.0 all-gather.22
  116.5 28.2 all-gather.20
  147.6 54.0 all-gather.16
  204.5 62.3 all-gather.24
  269.7 61.8 all-gather.26
  393.4 24.4 reduce-scatter.19
  465.0 24.6 reduce-scatter.21
  550.8 58.5 all-gather.18
  615.1 27.1 all-gather.22
  643.9 28.2 all-gather.20
  675.0 53.9 all-gather.16
  731.9 62.4 all-gather.24
  797.2 61.8 all-gather.26
  920.9 24.4 reduce-scatter.19
  992.6 24.6 reduce-scatter.21
Sparse Core Ops, SparseCore 1:
  1092.2 117.5 all-reduce.40
  1215.1 96.7 reduce-scatter.17
  1317.6 98.7 reduce-scatter.11
  1422.6 118.4 reduce-scatter.9
  1547.6 135.2 reduce-scatter.13
  1689.3 135.1 reduce-scatter.15
where the time goes:
time: 1840 us; the launch traced here: 1830 us
  waiting for transfers between devices  937 us (51%)
  matrix products  470 us (26%)
  blocking collectives  288 us (16%)
  local copies, waits for them, and re-layouts  63.9 us (3%)
  other arithmetic  49.7 us (3%)
    all_gather x2, blocking collectives, one_sequence(): lax.all_gather(reduce_weight, ('dp', 'ctx'), axis=0, tiled=True)  147 us
    reduce_scatter x1, waiting for transfers between devices, shards(): lax.psum_scatter(totals[7], ('dp', 'ctx'), scatter_dimension=0, tiled=True)  142 us
    reduce_scatter x1, waiting for transfers between devices, shards(): lax.psum_scatter(totals[9], ('dp', 'ctx'), scatter_dimension=0, tiled=True)  142 us
    reduce_scatter x1, waiting for transfers between devices, shards(): lax.psum_scatter(totals[0], ('dp', 'ctx'), scatter_dimension=0, tiled=True)  125 us
    all_gather x2, waiting for transfers between devices, one_sequence(): lax.all_gather(in_weight, ('dp', 'ctx'), axis=0, tiled=True)  119 us
    dot_general x2, matrix products, attend_back(): jnp.einsum('ghqk,gqhe->gkhe', grad_scores, queries, preferred_element_typ...  108 us
    dot_general x2, matrix products, attend_back(): jnp.einsum('ghqk,gkhe->gqhe', grad_scores, keys, preferred_element_type=j...  108 us
    unnamed x7, waiting for transfers between devices  106 us
  transfers between devices with their start and end apart: 22, of which 12 were waited for; matrix products, arithmetic and copies ran while one was open for 23% of the time, Pallas kernels for 0%

commit v1 on v0

v1 whole, which is shorter than its diff:
```python
from functools import partial

import jax
import jax.numpy as jnp
from jax import lax
from jax.sharding import PartitionSpec as P

H = 12
HD = 64
RED = 128
PH = 2
CLS = 14


negative = -1e30
epsilon = 1e-06
highest = lax.Precision.HIGHEST


def exchange(value, axis):
    size = lax.axis_size(axis)
    me = lax.axis_index(axis)
    result = value
    for step in range(1, size):
        other = (me + step) % size
        source = (me - step) % size
        sent = lax.dynamic_index_in_dim(value, other, 0, keepdims=False)
        came = lax.ppermute(sent, axis, [(k, (k + step) % size) for k in range(size)])
        result = lax.dynamic_update_index_in_dim(result, came, source, 0)
    return result


def summed_everywhere(value):
    for axis in ("dp", "ctx"):
        size = lax.axis_size(axis)
        step = 1
        while step < size:
            value = value + lax.ppermute(value, axis, [(k, k ^ step) for k in range(size)])
            step *= 2
    return value


def everyone(value):
    return lax.all_gather(value, ("dp", "ctx"), axis=0, tiled=True)


def to_owners(value):
    return lax.psum_scatter(value, ("dp", "ctx"), scatter_dimension=0, tiled=True)


def norm_rows(hidden, gain, shift):
    average = jnp.mean(hidden, axis=-1, keepdims=True)
    centred = hidden - average
    inv_std = lax.rsqrt(jnp.mean(centred * centred, axis=-1, keepdims=True) + epsilon)
    normed = centred * inv_std
    return (normed * gain + shift, normed, inv_std)


def norm_back(upstream, normed, inv_std, gain):
    scaled = upstream * gain
    first_mean = jnp.mean(scaled, axis=-1, keepdims=True)
    second = jnp.mean(scaled * normed, axis=-1, keepdims=True)
    return inv_std * (scaled - first_mean - normed * second)


def rows_product(left, right, precision=None):
    return lax.dot_general(
        left,
        right,
        (((0,), (0,)), ((), ())),
        precision=precision,
        preferred_element_type=jnp.float32,
    )


def right_transposed(left, right, precision=None):
    return lax.dot_general(
        left,
        right,
        (((1,), (1,)), ((), ())),
        precision=precision,
        preferred_element_type=jnp.float32,
    )


def piece_labels(positions, starts, lengths):
    inside = (positions[None, :, None] >= starts[:, None, :]) & (
        positions[None, :, None] < (starts + lengths)[:, None, :]
    )
    labels = jnp.arange(1, starts.shape[1] + 1, dtype=jnp.int32)
    return jnp.sum(jnp.where(inside, labels, 0), axis=2) - 1


def allowed_pairs(query_pos, key_pos, starts, lengths):
    query_label = piece_labels(query_pos, starts, lengths)
    key_label = piece_labels(key_pos, starts, lengths)
    causal = key_pos[None, None, :] <= query_pos[None, :, None]
    together = (query_label[:, :, None] == key_label[:, None, :]) & (query_label[:, :, None] >= 0)
    return (causal | together)[:, None]


def scores_of(queries, keys, allowed):
    raw_scores = (
        jnp.einsum("gqhe,gkhe->ghqk", queries, keys, preferred_element_type=jnp.float32) * 0.125
    )
    return jnp.where(allowed, raw_scores, negative)


def attend_block(query_pos, key_pos, inputs):
    queries, keys, values, starts, lengths = inputs
    scores = scores_of(queries, keys, allowed_pairs(query_pos, key_pos, starts, lengths))
    row_top = jnp.max(scores, axis=-1, keepdims=True)
    row_total = jnp.sum(jnp.exp(scores - row_top), axis=-1, keepdims=True)
    log_total = row_top + jnp.log(row_total)
    prob_low = jnp.exp(scores - log_total).astype(jnp.bfloat16)
    mixed_block = jnp.einsum(
        "ghqk,gkhe->gqhe", prob_low, values, preferred_element_type=jnp.float32
    )
    return (mixed_block.astype(jnp.bfloat16), log_total[..., 0])


def score_grads(
    query_pos, key_pos, queries, keys, values, starts, lengths, log_total, grad_mixed, centre
):
    scores = scores_of(queries, keys, allowed_pairs(query_pos, key_pos, starts, lengths))
    prob_full = jnp.exp(scores - log_total[..., None])
    grad_probs = jnp.einsum(
        "gqhe,gkhe->ghqk", grad_mixed, values, preferred_element_type=jnp.float32
    )
    centre = jnp.sum(prob_full * grad_probs, axis=-1)
    grad_scores = (prob_full * (grad_probs - centre[..., None]) * 0.125).astype(jnp.bfloat16)
    return (prob_full, grad_scores, centre)


def attend_back(query_pos, key_pos, inputs):
    queries, keys, values, starts, lengths, log_total, grad_mixed = inputs
    prob_full, grad_scores, centre = score_grads(
        query_pos, key_pos, queries, keys, values, starts, lengths, log_total, grad_mixed, None
    )
    grad_queries = jnp.einsum(
        "ghqk,gkhe->gqhe", grad_scores, keys, preferred_element_type=jnp.float32
    )
    grad_keys = jnp.einsum(
        "ghqk,gqhe->gkhe", grad_scores, queries, preferred_element_type=jnp.float32
    )
    grad_values = jnp.einsum(
        "ghqk,gqhe->gkhe",
        prob_full.astype(jnp.bfloat16),
        grad_mixed,
        preferred_element_type=jnp.float32,
    )
    return (grad_queries, grad_keys, grad_values)


def attention(positions, qkv_low, starts, lengths):
    length, width = qkv_low.shape[0], qkv_low.shape[1] // 3
    queries, keys, values = [
        qkv_low[:, k * width : (k + 1) * width].reshape(1, length, H, HD) for k in range(3)
    ]
    mixed, log_total = attend_block(positions, positions, (queries, keys, values, starts, lengths))
    return mixed.reshape(length, width), log_total


def attention_back(positions, qkv_low, starts, lengths, log_total, mixed_low, grad_mixed_low):
    length, width = mixed_low.shape
    queries, keys, values = [
        qkv_low[:, k * width : (k + 1) * width].reshape(1, length, H, HD) for k in range(3)
    ]
    grads = attend_back(
        positions,
        positions,
        (
            queries,
            keys,
            values,
            starts,
            lengths,
            log_total,
            grad_mixed_low.reshape(1, length, H, HD),
        ),
    )
    return jnp.concatenate(
        [grad.reshape(length, width).astype(jnp.bfloat16) for grad in grads], axis=1
    )


def interleave(rows, devices):
    width = rows.shape[1]
    part = rows.shape[0] // (4 * devices)
    split = rows.reshape(devices, 4, part, width)
    return jnp.swapaxes(split, 1, 2).reshape(devices * part, 4 * width)


def separate(columns, devices):
    width = columns.shape[1] // 4
    part = columns.shape[0] // devices
    split = columns.reshape(devices, part, 4, width)
    return jnp.swapaxes(split, 1, 2).reshape(devices * 4 * part, width)


def vector_columns(vectors, hidden_vector, devices):
    columns = [vector[:, None] for vector in vectors]
    columns.append(interleave(hidden_vector[:, None], devices))
    packed = jnp.concatenate(columns, axis=1)
    return jnp.pad(packed, ((0, 0), (0, 128 - packed.shape[1])))


def shards(
    tokens,
    out_grad,
    logit_grad,
    piece_start,
    piece_len,
    qkv_weight,
    query_bias,
    value_bias,
    out_weight,
    out_bias,
    gain_one,
    shift_one,
    in_weight,
    in_bias,
    back_weight,
    back_bias,
    gain_two,
    shift_two,
    reduce_weight,
    reduce_bias,
    pool_query,
    pool_weight,
    pool_bias,
    class_weight,
    class_bias,
):
    seq_count, local_len, width = tokens.shape
    ctx_size = lax.axis_size("ctx")
    assert seq_count == ctx_size
    devices = lax.axis_size("dp") * ctx_size
    hidden_units = in_weight.shape[1]
    assert hidden_units == 4 * width
    full_len = local_len * ctx_size
    head_width = RED // PH
    mine = lax.axis_index("ctx")
    positions = jnp.arange(full_len, dtype=jnp.int32)
    query_rows = pool_query.astype(jnp.float32).reshape(PH, head_width)
    pool_weight_f = pool_weight.astype(jnp.float32)
    class_weight_f = class_weight.astype(jnp.float32)
    reduce_shift = reduce_bias.astype(jnp.float32)
    pool_shift = pool_bias.astype(jnp.float32)
    class_shift = class_bias.astype(jnp.float32)
    starts = lax.dynamic_slice_in_dim(piece_start, mine, 1, 0)
    lengths = lax.dynamic_slice_in_dim(piece_len, mine, 1, 0)
    logit_row = lax.dynamic_slice_in_dim(logit_grad, mine, 1, 0)

    small = vector_columns(
        (query_bias, value_bias, out_bias, gain_one, shift_one, back_bias, gain_two, shift_two),
        in_bias,
        1,
    )
    early = everyone(jnp.concatenate([qkv_weight, small], axis=1))
    late = everyone(
        jnp.concatenate(
            [out_weight, in_weight, interleave(back_weight, 1), reduce_weight], axis=1
        )
    )
    seq_tokens = exchange(tokens, "ctx").reshape(full_len, width)
    seq_out_grad = exchange(out_grad, "ctx").reshape(full_len, width)

    qkv_full = early[:, : 3 * width]
    vectors = early[:, 3 * width :].astype(jnp.float32)
    q_bias, v_bias, o_bias, g_one, s_one, b_bias, g_two, s_two = [vectors[:, k] for k in range(8)]
    i_bias = separate(vectors[:, 8:12], devices)[:, 0]
    out_full = late[:, :width]
    in_full = late[:, width : 5 * width]
    back_full = separate(late[:, 5 * width : 9 * width], devices)
    reduce_full = late[:, 9 * width :]

    qkv_shift = jnp.concatenate([q_bias, jnp.zeros_like(q_bias), v_bias])
    qkv_low = (
        jnp.dot(seq_tokens, qkv_full, preferred_element_type=jnp.float32) + qkv_shift
    ).astype(jnp.bfloat16)
    mixed_low, log_total = attention(positions, qkv_low, starts, lengths)
    attended = jnp.dot(mixed_low, out_full, preferred_element_type=jnp.float32) + o_bias
    first_norm, normed_one, inv_one = norm_rows(
        seq_tokens.astype(jnp.float32) + attended, g_one, s_one
    )
    first_low = first_norm.astype(jnp.bfloat16)
    inner_pre = jnp.dot(first_low, in_full, preferred_element_type=jnp.float32) + i_bias
    active, gelu_back = jax.vjp(partial(jax.nn.gelu, approximate=False), inner_pre)
    active_low = active.astype(jnp.bfloat16)
    branch = jnp.dot(active_low, back_full, preferred_element_type=jnp.float32) + b_bias
    result, normed_two, inv_two = norm_rows(first_norm + branch, g_two, s_two)
    result_low = result.astype(jnp.bfloat16)
    layer_out = exchange(result_low.reshape(ctx_size, local_len, width), "ctx")
    reduced = jnp.dot(result_low, reduce_full, preferred_element_type=jnp.float32) + reduce_shift
    pool_heads = reduced.reshape(full_len, PH, head_width)
    pool_scores = jnp.einsum("lpe,pe->lp", pool_heads, query_rows, precision=highest) * 0.125
    pool_top = jnp.max(pool_scores, axis=0)
    pool_exp = jnp.exp(pool_scores - pool_top)
    pool_total = jnp.sum(pool_exp, axis=0)
    pool_probs = pool_exp / pool_total
    pooled_heads = jnp.einsum("lp,lpe->pe", pool_probs, pool_heads, precision=highest)
    pooled = pooled_heads.reshape(1, RED)
    hidden = jnp.tanh(jnp.dot(pooled, pool_weight_f, precision=highest) + pool_shift)
    logit_mine = jnp.dot(hidden, class_weight_f, precision=highest) + class_shift
    logits = exchange(jnp.broadcast_to(logit_mine[None], (ctx_size, 1, CLS)), "ctx")[:, 0]

    grad_class = rows_product(hidden, logit_row, highest)
    grad_class_bias = jnp.sum(logit_row, axis=0)
    grad_hidden = right_transposed(logit_row, class_weight_f, highest)
    grad_pre = grad_hidden * (1.0 - hidden * hidden)
    grad_pool_weight = rows_product(pooled, grad_pre, highest)
    grad_pool_bias = jnp.sum(grad_pre, axis=0)
    grad_pooled = right_transposed(grad_pre, pool_weight_f, highest).reshape(PH, head_width)
    pool_along = jnp.einsum(
        "lpe,pe->lp", pool_heads, grad_pooled, precision=highest
    ) - jnp.sum(pooled_heads * grad_pooled, axis=-1)
    grad_pool_scores = pool_probs * pool_along
    grad_reduced = (
        pool_probs[..., None] * grad_pooled + grad_pool_scores[..., None] * query_rows * 0.125
    )
    grad_query = (
        jnp.einsum("lp,lpe->pe", grad_pool_scores, pool_heads, precision=highest).reshape(RED)
        * 0.125
    )
    grad_red_low = grad_reduced.reshape(full_len, RED).astype(jnp.bfloat16)
    grad_reduce_bias = jnp.sum(grad_red_low.astype(jnp.float32), axis=0)
    tiny = summed_everywhere(
        jnp.concatenate(
            [
                grad_pool_weight,
                jnp.pad(grad_class.T, ((0, 16 - CLS), (0, 0))),
                jnp.pad(grad_class_bias, (0, RED - CLS))[None],
                grad_pool_bias[None],
                grad_query[None],
                grad_reduce_bias[None],
                jnp.zeros((4, RED), jnp.float32),
            ],
            axis=0,
        )
    )
    grad_reduce = rows_product(result_low, grad_red_low)
    grad_result = seq_out_grad.astype(jnp.float32) + right_transposed(grad_red_low, reduce_full)
    grad_gain_two = jnp.sum(grad_result * normed_two, axis=0)
    grad_shift_two = jnp.sum(grad_result, axis=0)
    grad_mid = norm_back(grad_result, normed_two, inv_two, g_two)
    grad_branch_low = grad_mid.astype(jnp.bfloat16)
    grad_back_bias = jnp.sum(grad_branch_low.astype(jnp.float32), axis=0)
    grad_back = rows_product(active_low, grad_branch_low)
    grad_active = right_transposed(grad_branch_low, back_full)
    grad_inner_low = gelu_back(grad_active)[0].astype(jnp.bfloat16)
    grad_in_bias = jnp.sum(grad_inner_low.astype(jnp.float32), axis=0)
    grad_in = rows_product(first_low, grad_inner_low)
    early_owned = to_owners(
        jnp.concatenate(
            [
                grad_in.astype(jnp.bfloat16),
                interleave(grad_back.astype(jnp.bfloat16), devices),
                grad_reduce.astype(jnp.bfloat16),
            ],
            axis=1,
        )
    ).astype(jnp.float32)
    grad_first = grad_mid + right_transposed(grad_inner_low, in_full)
    grad_gain_one = jnp.sum(grad_first * normed_one, axis=0)
    grad_shift_one = jnp.sum(grad_first, axis=0)
    grad_start = norm_back(grad_first, normed_one, inv_one, g_one)
    grad_attn_low = grad_start.astype(jnp.bfloat16)
    grad_out_bias = jnp.sum(grad_attn_low.astype(jnp.float32), axis=0)
    grad_out = rows_product(mixed_low, grad_attn_low)
    grad_mixed_low = right_transposed(grad_attn_low, out_full).astype(jnp.bfloat16)
    grad_qkv_low = attention_back(
        positions, qkv_low, starts, lengths, log_total, mixed_low, grad_mixed_low
    )
    grad_query_bias = jnp.sum(grad_qkv_low[:, :width].astype(jnp.float32), axis=0)
    grad_value_bias = jnp.sum(grad_qkv_low[:, 2 * width :].astype(jnp.float32), axis=0)
    grad_qkv = rows_product(seq_tokens, grad_qkv_low)
    grad_small = vector_columns(
        (
            grad_query_bias,
            grad_value_bias,
            grad_out_bias,
            grad_gain_one,
            grad_shift_one,
            grad_back_bias,
            grad_gain_two,
            grad_shift_two,
        ),
        grad_in_bias,
        devices,
    )
    late_owned = to_owners(
        jnp.concatenate(
            [
                grad_qkv.astype(jnp.bfloat16),
                grad_out.astype(jnp.bfloat16),
                grad_small.astype(jnp.bfloat16),
            ],
            axis=1,
        )
    ).astype(jnp.float32)
    token_grad = (grad_start + right_transposed(grad_qkv_low, qkv_full)).astype(jnp.bfloat16)
    token_grad = exchange(token_grad.reshape(ctx_size, local_len, width), "ctx")
    small_owned = late_owned[:, 4 * width :]
    tall = RED + 16
    return (
        layer_out,
        logits,
        token_grad,
        late_owned[:, : 3 * width],
        small_owned[:, 0],
        small_owned[:, 1],
        late_owned[:, 3 * width : 4 * width],
        small_owned[:, 2],
        small_owned[:, 3],
        small_owned[:, 4],
        early_owned[:, : 4 * width],
        separate(small_owned[:, 8:12], 1)[:, 0],
        separate(early_owned[:, 4 * width : 8 * width], 1),
        small_owned[:, 5],
        small_owned[:, 6],
        small_owned[:, 7],
        early_owned[:, 8 * width :],
        tiny[tall + 3],
        tiny[tall + 2],
        tiny[:RED],
        tiny[tall + 1],
        tiny[RED : RED + CLS].T,
        tiny[tall, :CLS],
    )


def solution(mesh):
    placed = (
        P("dp", "ctx", None),
        P("dp", "ctx", None),
        P("dp", None),
        P("dp", None),
        P("dp", None),
        P(("dp", "ctx"), None),
        P(("dp", "ctx")),
        P(("dp", "ctx")),
        P(("dp", "ctx"), None),
        P(("dp", "ctx")),
        P(("dp", "ctx")),
        P(("dp", "ctx")),
        P(("dp", "ctx"), None),
        P(("dp", "ctx")),
        P(("dp", "ctx"), None),
        P(("dp", "ctx")),
        P(("dp", "ctx")),
        P(("dp", "ctx")),
        P(("dp", "ctx"), None),
        P(),
        P(),
        P(),
        P(),
        P(),
        P(),
    )
    return jax.shard_map(
        shards,
        mesh=mesh,
        in_specs=placed,
        out_specs=(
            P("dp", "ctx", None),
            P("dp", None),
            P("dp", "ctx", None),
            P(("dp", "ctx"), None),
            P(("dp", "ctx")),
            P(("dp", "ctx")),
            P(("dp", "ctx"), None),
            P(("dp", "ctx")),
            P(("dp", "ctx")),
            P(("dp", "ctx")),
            P(("dp", "ctx"), None),
            P(("dp", "ctx")),
            P(("dp", "ctx"), None),
            P(("dp", "ctx")),
            P(("dp", "ctx")),
            P(("dp", "ctx")),
            P(("dp", "ctx"), None),
            P(),
            P(),
            P(),
            P(),
            P(),
            P(),
        ),
        check_vma=False,
    )
```

time: 1840 us -> 731 us (0.40)
  waiting for transfers between devices: 937 us -> 242 us
  blocking collectives: 288 us -> 0 us
  matrix products: 470 us -> 345 us
    reduce_scatter x8 -> x0, waiting for transfers between devices: 513 us -> none  [the longest x1 142 us: shards(): lax.psum_scatter(totals[7], ('dp', 'ctx'), scatter_dimension=0, tiled=True)]
    all_gather x12 -> x2, waiting for transfers between devices: 238 us -> 25.9 us  [everyone(): return lax.all_gather(value, ('dp', 'ctx'), axis=0, tiled=True)]
    all_gather x4 -> x0, blocking collectives: 155 us -> none  [the longest x2 147 us: one_sequence(): lax.all_gather(reduce_weight, ('dp', 'ctx'), axis=0, tiled=True)]
    while x4 -> x0, blocking collectives: 92.4 us -> none
    psum x1 -> x0, waiting for transfers between devices: 74.3 us -> none  [shards(): lax.psum((totals[14], totals[15], totals[16], totals[17], totals[18], tot...]
    ppermute x0 -> x10, waiting for transfers between devices: none -> 67.1 us  [the longest x5 49.4 us: exchange(): lax.ppermute(sent, axis, [(k, (k + step) % size) for k in range(size)])]
    unnamed x7 -> x6, waiting for transfers between devices: 106 us -> 149 us
    dot_general x2 -> x1, matrix products: 108 us -> 64.8 us  [attend_back(): jnp.einsum('ghqk,gkhe->gqhe', grad_scores, keys, preferred_element_type=j...]
  transfers between devices with their start and end apart: 22 -> 14, of which waited for: 12 -> 11; matrix products, arithmetic and copies ran while one was open for 23% -> 20% of each run, Pallas kernels for 0% -> 0%
where the time goes in v1:
time: 731 us; the launch traced here: 724 us
  matrix products  345 us (47%)
  waiting for transfers between devices  242 us (33%)
  local copies, waits for them, and re-layouts  67.1 us (9%)
  other arithmetic  43.4 us (6%)
  between operations  15.6 us (2%)
  starting transfers between devices  11.2 us (2%)
    unnamed x6, waiting for transfers between devices  149 us
    dot_general x1, matrix products, attend_back(): jnp.einsum('ghqk,gqhe->gkhe', grad_scores, queries, preferred_element_typ...  66 us
    dot_general x1, matrix products, attend_back(): jnp.einsum('ghqk,gkhe->gqhe', grad_scores, keys, preferred_element_type=j...  64.8 us
    ppermute x5, waiting for transfers between devices, exchange(): lax.ppermute(sent, axis, [(k, (k + step) % size) for k in range(size)])  49.4 us
    dot_general x7, matrix products, right_transposed(): lax.dot_general(left, right, (((1,), (1,)), ((), ())), precision=precisio...  44.6 us
    dot_general x1, matrix products, shards(): jnp.dot(first_low, in_full, preferred_element_type=jnp.float32) + i_bias  36.8 us
    dot_general x5, matrix products, rows_product(): lax.dot_general(left, right, (((0,), (0,)), ((), ())), precision=precisio...  27.4 us
    all_gather x2, waiting for transfers between devices, everyone(): return lax.all_gather(value, ('dp', 'ctx'), axis=0, tiled=True)  25.9 us
  transfers between devices with their start and end apart: 14, of which 11 were waited for; matrix products, arithmetic and copies ran while one was open for 20% of the time, Pallas kernels for 0%

profile of v1, /device:TPU:0, one launch (start us, length us, event | category | flops | bytes accessed | tf_op | source)
XLA Modules:
  0.0 724.4 jit_solution(11778635766592037136)
XLA Ops:
  22.4 15.9 %collective-permute-done = bf16[512,768]{1,0:T(8,128)(2,1)} collective-permute-done((bf16[512,768]{1,0:T(8,128)(2,1)}, bf16[512,768]{1,0:T(8,128)(2,1)}, u32[]{:S(2)}, u32[]{:S(2)}) %collective-permute-start) | collective-permute-done | bytes 786464 | tf_op jit(solution)/shard_map/ppermute | solution.py:28
  40.4 17.3 %collective-permute-done.3 = bf16[512,768]{1,0:T(8,128)(2,1)} collective-permute-done((bf16[512,768]{1,0:T(8,128)(2,1)}, bf16[512,768]{1,0:T(8,128)(2,1)}, u32[]{:S(2)}, u32[]{:S(2)}) %collective-permute-start.3) | collective-permute-done | bytes 786464 | tf_op jit(solution)/shard_map/ppermute | solution.py:28
  58.8 20.3 %all-gather.3.cloned.1.call-done = bf16[768,2432]{1,0:T(8,128)(2,1)} async-done(((bf16[24,2432]{1,0:T(8,128)(2,1)}), bf16[768,2432]{1,0:T(8,128)(2,1)}) %all-gather.3.cloned.1.call-update) | async-done | bytes 3735568 | tf_op jit(solution)/shard_map/all_gather | solution.py:44
  82.4 6.3 add_convert_fusion.1
  90.7 3.1 copy.154
  97.1 22.4 %fusion.2 = (f32[12,1024]{1,0:T(8,128)S(1)}, f32[12,1024,1024]{1,2,0:T(8,128)}) fusion(pred[1024,1024]{0,1:T(8,128)(4,1)S(1)} %fusion.36, bf16[1024,12,64]{0,2,1:T(8,128)(2,1)} %bitcast.222, bf16[1024,12,64]{0,2,1:T(8,128)(2,1)} %bitcast.220), kind=kOutput, calls=%fused_computation.7 | convolution fusion | flops 1648349184 | bytes 54575104 | tf_op jit(solution)/shard_map/gqhe,gkhe->ghqk/dot_general | solution.py:104
  119.5 21.9 %exponential_reduce_fusion = f32[12,1024]{1,0:T(8,128)S(1)} fusion(f32[12,1024,1024]{1,2,0:T(8,128)} %get-tuple-element.64, f32[12,1024]{1,0:T(8,128)S(1)} %get-tuple-element.63, pred[1024,1024]{0,1:T(8,128)(4,1)S(1)} %fusion.36), kind=kLoop, calls=%fused_computation.5 | loop fusion | flops 50319360 | bytes 51478528 | tf_op jit(solution)/shard_map/reduce_sum | solution.py:113
  141.5 21.0 %convolution_convert_fusion.5 = bf16[12,64,1024]{2,1,0:T(8,128)(2,1)} fusion(bf16[1024,12,64]{0,2,1:T(8,128)(2,1)S(1)} %bitcast.218, f32[12,1024,1024]{1,2,0:T(8,128)} %get-tuple-element.64, f32[12,1024]{1,0:T(8,128)S(1)} %log_add_fusion, pred[1024,1024]{0,1:T(8,128)(4,1)S(1)} %fusion.36), kind=kOutput, calls=%fused_computation.78 | convolution fusion | flops 1661730816 | bytes 54575104 | tf_op jit(solution)/shard_map/ghqk,gkhe->gqhe/dot_general | solution.py:116
  162.6 5.6 all-gather.5.cloned.1.call-done
  168.2 4.9 slice.178
  173.1 9.9 %reshape.545 = bf16[32,24,4,768]{3,2,1,0:T(4,128)(2,1)} reshape(bf16[768,3072]{1,0:T(8,128)(2,1)} %slice.178) | data formatting | bytes 9437184 | tf_op jit(solution)/shard_map/reshape | solution.py:197
  183.0 3.4 copy.158
  186.4 3.9 fusion.114
  190.9 36.8 %multiply_convert_fusion.1 = (bf16[1024,3072]{1,0:T(8,128)(2,1)S(1)}, f32[1024,3072]{1,0:T(8,128)}, f32[1024,3072]{1,0:T(8,128)}) fusion(f32[3072]{0:T(1024)S(1)} %add.239, bf16[768,7040]{1,0:T(8,128)(2,1)} %all-gather.5.cloned.1.call-done, f32[1024,768]{1,0:T(8,128)S(1)} %get-tuple-element.66, f32[768]{0:T(1024)S(1)} %get-tuple-element.34, ...), kind=kOutput, calls=%fused_computation.22 | convolution fusion | flops 5043388416 | bytes 39348224 | tf_op jit(solution)/shard_map/dot_general | solution.py:288
  227.7 5.5 fusion.115
  242.3 4.0 multiply_reduce_fusion.1
  249.1 19.3 %fusion.120 = (bf16[3072]{0:T(1024)(128)(2,1)S(1)}, bf16[1024,3072]{1,0:T(8,128)(2,1)}) fusion(f32[1024,3072]{1,0:T(8,128)} %get-tuple-element.52, bf16[3072,768]{1,0:T(8,128)(2,1)} %bitcast.225, f32[1024,768]{1,0:T(8,128)} %get-tuple-element.48, f32[1024,3072]{1,0:T(8,128)} %get-tuple-element.67, f32[3072]{0:T(1024)S(1)} %add.239), kind=kOutput, calls=%fused_computation.201 | convolution fusion | flops 4882953216 | bytes 39340032 | tf_op jit(solution)/shard_map/dot_general | solution.py:77
  268.4 10.1 %multiply_reduce_fusion.2 = (bf16[768]{0:T(1024)(128)(2,1)S(1)}, f32[1024]{0:T(1024)S(1)}, f32[1024]{0:T(1024)S(1)}, bf16[768]{0:T(1024)(128)(2,1)S(1)}, f32[1024,768]{1,0:T(8,128)S(1)}) fusion(f32[1024,768]{1,0:T(8,128)S(1)} %copy-done.10, f32[1024]{0:T(1024)S(1)} %add_rsqrt_fusion.1, f32[1024]{0:T(1024)S(1)} %broadcast_multiply_fusion.7, ...), kind=kOutput, calls=%fused_computation.53 | convolution fusion | flops 4839698432 | bytes 20469760 | tf_op jit(solution)/shard_map/dot_general | solution.py:77
  286.4 21.1 %fusion.119 = (bf16[12,64]{1,0:T(8,128)(2,1)S(1)}, bf16[12,64,1024]{2,1,0:T(8,128)(2,1)}) fusion(bf16[1024,12,64]{0,2,1:T(8,128)(2,1)S(1)} %bitcast.230, f32[12,1024,1024]{1,2,0:T(8,128)} %get-tuple-element.64, f32[12,1024]{1,0:T(8,128)S(1)} %copy-done.33, pred[1024,1024]{0,1:T(8,128)(4,1)S(1)} %copy-done.6), kind=kOutput, calls=%fused_computation.200 | convolution fusion | flops 1662516480 | bytes 54576640 | tf_op jit(solution)/shard_map/ghqk,gqhe->gkhe/dot_general | solution.py:146
  307.5 20.7 %fusion.123 = f32[12,1024,1024]{1,2,0:T(8,128)} fusion(bf16[1024,12,64]{0,2,1:T(8,128)(2,1)} %bitcast.231, bf16[1024,12,64]{0,2,1:T(8,128)(2,1)S(1)} %bitcast.219), kind=kOutput, calls=%fused_computation.204 | convolution fusion | flops 1610612736 | bytes 53477376 | tf_op jit(solution)/shard_map/gqhe,gkhe->ghqk/dot_general | solution.py:127
  328.2 66.0 %fusion.51 = bf16[12,64,1024]{2,1,0:T(8,128)(2,1)} fusion(bf16[1024,12,64]{0,2,1:T(8,128)(2,1)} %bitcast.223, f32[12,1024,1024]{1,2,0:T(8,128)} %fusion.123, f32[12,1024,1024]{1,2,0:T(8,128)} %get-tuple-element.64, f32[12,1024]{1,0:T(8,128)S(1)} %copy-done.33, pred[1024,1024]{0,1:T(8,128)(4,1)S(1)} %copy-done.6), kind=kOutput, calls=%fused_computation.75 | convolution fusion | flops 1749824512 | bytes 104906752 | tf_op jit(solution)/shard_map/ghqk,gqhe->gkhe/dot_general | solution.py:143
  394.3 64.8 %fusion.116 = (bf16[12,64]{1,0:T(8,128)(2,1)S(1)}, bf16[12,64,1024]{2,1,0:T(8,128)(2,1)}) fusion(bf16[1024,12,64]{0,2,1:T(8,128)(2,1)S(1)} %bitcast.221, f32[12,1024,1024]{1,2,0:T(8,128)} %fusion.123, f32[12,1024,1024]{1,2,0:T(8,128)} %get-tuple-element.64, f32[12,1024]{1,0:T(8,128)S(1)} %copy-done.33, pred[1024,1024]{0,1:T(8,128)(4,1)S(1)} %copy-done.6), kind=kOutput, calls=%fused_computation.199 | convolution fusion | flops 1750610176 | bytes 104908288 | tf_op jit(solution)/shard_map/ghqk,gkhe->gqhe/dot_general | solution.py:140
  459.8 6.8 convolution_convert_fusion.2
  471.1 8.9 %convolution_convert_fusion = bf16[3072,768]{1,0:T(8,128)(2,1)S(1)} fusion(bf16[1024,3072]{1,0:T(8,128)(2,1)} %copy-done.78, f32[1024,768]{1,0:T(8,128)S(1)} %copy-done.19), kind=kOutput, calls=%fused_computation.40 | convolution fusion | flops 4834983936 | bytes 14155776 | tf_op jit(solution)/shard_map/dot_general | solution.py:67
  485.0 8.7 %convolution_convert_fusion.1 = bf16[768,3072]{1,0:T(8,128)(2,1)S(1)} fusion(bf16[1024,3072]{1,0:T(8,128)(2,1)} %get-tuple-element.77, f32[1024,768]{1,0:T(8,128)S(1)} %copy-done.11, f32[768]{0:T(1024)S(1)} %copy-done.42, f32[768]{0:T(1024)S(1)} %get-tuple-element.35, f32[1024]{0:T(1024)S(1)} %add_rsqrt_fusion.1, f32[1024]{0:T(1024)S(1)} %broadcast_multiply_fusion.7), kind=kOutput, calls=%fused_computation.41 | convolution fusion | flops 4838129664 | bytes 14170112 | tf_op jit(solution)/shard_map/dot_general | solution.py:67
  493.7 6.5 pad_maximum_fusion
  511.1 4.7 collective-permute-done.7
  516.4 8.2 %add_convert_fusion.2 = bf16[1024,768]{1,0:T(8,128)(2,1)S(1)} fusion(f32[1024,768]{1,0:T(8,128)} %copy-done.18, bf16[768,2432]{1,0:T(8,128)(2,1)} %all-gather.3.cloned.1.call-done, bf16[1024,768]{0,1:T(8,128)(2,1)} %bitcast.261, bf16[1024,768]{0,1:T(8,128)(2,1)} %bitcast.263, bf16[1024,768]{0,1:T(8,128)(2,1)} %bitcast.265), kind=kOutput, calls=%fused_computation.54 | convolution fusion | flops 3639607296 | bytes 12976128 | tf_op jit(solution)/shard_map/dot_general | solution.py:77
  528.2 9.5 %collective-permute-done.9 = f32[152,128]{1,0:T(8,128)S(1)} collective-permute-done((f32[152,128]{1,0:T(8,128)S(1)}, f32[152,128]{1,0:T(8,128)S(1)}, u32[]{:S(2)}, u32[]{:S(2)}) %collective-permute-start.9) | collective-permute-done | bytes 77856 | tf_op jit(solution)/shard_map/ppermute | solution.py:38
  540.0 16.2 %collective-permute-done.4 = bf16[512,768]{1,0:T(8,128)(2,1)} collective-permute-done((bf16[512,768]{1,0:T(8,128)(2,1)}, bf16[512,768]{1,0:T(8,128)(2,1)}, u32[]{:S(2)}, u32[]{:S(2)}) %collective-permute-start.4) | collective-permute-done | bytes 786464 | tf_op jit(solution)/shard_map/ppermute | solution.py:28
  558.2 19.2 %reduce-scatter.7.cloned.1.call-done = bf16[24,3200]{1,0:T(8,128)(2,1)} async-done(((bf16[768,3200]{1,0:T(8,128)(2,1)}), bf16[24,3200]{1,0:T(8,128)(2,1)}) %reduce-scatter.7.cloned.1.call-update) | async-done | bytes 153616
  583.7 129.7 %reduce-scatter.9.cloned.1.call-done = bf16[24,6272]{1,0:T(8,128)(2,1)} async-done(((bf16[768,6272]{1,0:T(8,128)(2,1)}), bf16[24,6272]{1,0:T(8,128)(2,1)}) %reduce-scatter.9.cloned.1.call-update) | async-done | bytes 301072
  (303 shorter events, 86.2 us)
Async XLA Ops:
  7.2 231.3 %copy-start = (bf16[128,128]{1,0:T(8,128)(2,1)S(1)}, bf16[128,128]{1,0:T(8,128)(2,1)}, u32[]{:S(2)}) copy-start(bf16[128,128]{1,0:T(8,128)(2,1)} %param.46) | copy-start | bytes 98308
  7.4 71.8 %all-gather.3.cloned.1.call-start = ((), (), s32[]{:S(2)}) async-start(), calls=%async_computation.2 | async-start | bytes 3852288 | tf_op jit(solution)/shard_map/all_gather | solution.py:44
  12.7 155.5 %all-gather.5.cloned.1.call-start = ((), (), s32[]{:S(2)}) async-start(), calls=%async_computation.3 | async-start | bytes 11151360 | tf_op jit(solution)/shard_map/all_gather | solution.py:44
  13.7 563.8 %reduce-scatter.7.cloned.1.call-start = ((), (), s32[]{:S(2)}) async-start(), calls=%async_computation.4 | async-start | bytes 5068800
  15.8 22.5 %collective-permute-start = (bf16[512,768]{1,0:T(8,128)(2,1)}, bf16[512,768]{1,0:T(8,128)(2,1)}, u32[]{:S(2)}, u32[]{:S(2)}) collective-permute-start(bf16[512,768]{1,0:T(8,128)(2,1)} %dynamic-slice_bitcast_fusion.3), channel_id=1, source_target_pairs={{0,1},{1,0},{2,3},{3,2},{4,5},{5,4},{6,7},{7,6},{8,9},{9,8},{10,11... | collective-permute-start | bytes 2359304 | tf_op jit(solution)/shard_map/ppermute | solution.py:28
  19.7 37.9 %collective-permute-start.3 = (bf16[512,768]{1,0:T(8,128)(2,1)}, bf16[512,768]{1,0:T(8,128)(2,1)}, u32[]{:S(2)}, u32[]{:S(2)}) collective-permute-start(bf16[512,768]{1,0:T(8,128)(2,1)} %dynamic-slice_bitcast_fusion.1), channel_id=1, source_target_pairs={{0,1},{1,0},{2,3},{3,2},{4,5},{5,4},{6,7},{7,6},{8,9},{9,8},{10,11... | collective-permute-start | bytes 2359304 | tf_op jit(solution)/shard_map/ppermute | solution.py:28
  22.4 119.1 %copy-start.5 = (pred[1024,1024]{0,1:T(8,128)(4,1)}, pred[1024,1024]{0,1:T(8,128)(4,1)S(1)}, u32[]{:S(2)}) copy-start(pred[1024,1024]{0,1:T(8,128)(4,1)S(1)} %fusion.36) | copy-start | bytes 3145732
  58.8 23.6 %copy-start.16 = (bf16[2,512,768]{2,1,0:T(8,128)(2,1)}, bf16[2,512,768]{2,1,0:T(8,128)(2,1)S(1)}, u32[]{:S(2)}) copy-start(bf16[2,512,768]{2,1,0:T(8,128)(2,1)S(1)} %bitcast_dynamic-update-slice_fusion.1) | copy-start | bytes 4718596
  82.4 145.3 %copy-start.41 = (f32[768]{0:T(1024)}, f32[768]{0:T(1024)S(1)}, u32[]{:S(2)}) copy-start(f32[768]{0:T(1024)S(1)} %get-tuple-element.34) | copy-start | bytes 9220
  97.1 44.4 %copy-start.12 = (bf16[1024,768]{0,1:T(8,128)(2,1)}, bf16[1024,768]{0,1:T(8,128)(2,1)S(1)}, u32[]{:S(2)}) copy-start(bf16[1024,768]{0,1:T(8,128)(2,1)S(1)} %copy.152) | copy-start | bytes 4718596
  141.5 21.1 %copy-start.32 = (f32[12,1024]{1,0:T(8,128)}, f32[12,1024]{1,0:T(8,128)S(1)}, u32[]{:S(2)}) copy-start(f32[12,1024]{1,0:T(8,128)S(1)} %log_add_fusion) | copy-start | bytes 147460
  186.4 41.3 %copy-start.15 = (bf16[32,4,24,768]{3,2,1,0:T(8,128)(2,1)}, bf16[32,4,24,768]{3,2,1,0:T(8,128)(2,1)S(1)}, u32[]{:S(2)}) copy-start(bf16[32,4,24,768]{3,2,1,0:T(8,128)(2,1)S(1)} %copy.158) | copy-start | bytes 14155780
  190.3 37.4 %copy-start.9 = (f32[1024,768]{1,0:T(8,128)}, f32[1024,768]{1,0:T(8,128)S(1)}, u32[]{:S(2)}) copy-start(f32[1024,768]{1,0:T(8,128)S(1)} %get-tuple-element.66) | copy-start | bytes 9437188
  190.8 36.9 %copy-start.43 = (f32[768]{0:T(1024)S(1)}, f32[768]{0:T(1024)}, u32[]{:S(2)}) copy-start(f32[768]{0:T(1024)} %get-tuple-element.33) | copy-start | bytes 9220
  249.1 19.3 %copy-start.10 = (f32[1024,768]{1,0:T(8,128)S(1)}, f32[1024,768]{1,0:T(8,128)}, u32[]{:S(2)}) copy-start(f32[1024,768]{1,0:T(8,128)} %copy-done.9) | copy-start | bytes 9437188
  286.4 21.1 %copy-start.13 = (bf16[1024,768]{0,1:T(8,128)(2,1)S(1)}, bf16[1024,768]{0,1:T(8,128)(2,1)}, u32[]{:S(2)}) copy-start(bf16[1024,768]{0,1:T(8,128)(2,1)} %copy-done.12) | copy-start | bytes 4718596
  328.2 66.0 %copy-start.14 = (bf16[1024,768]{0,1:T(8,128)(2,1)S(1)}, bf16[1024,768]{0,1:T(8,128)(2,1)}, u32[]{:S(2)}) copy-start(bf16[1024,768]{0,1:T(8,128)(2,1)} %copy.154) | copy-start | bytes 4718596
  394.3 64.8 %copy-start.53 = (bf16[768]{0:T(1024)(128)(2,1)S(1)}, bf16[768]{0:T(1024)(128)(2,1)}, u32[]{:S(2)}) copy-start(bf16[768]{0:T(1024)(128)(2,1)} %get-tuple-element.23) | copy-start | bytes 4612
  394.3 64.8 %copy-start.52 = (bf16[768]{0:T(1024)(128)(2,1)S(1)}, bf16[768]{0:T(1024)(128)(2,1)}, u32[]{:S(2)}) copy-start(bf16[768]{0:T(1024)(128)(2,1)} %get-tuple-element.29) | copy-start | bytes 4612
  394.3 64.8 %copy-start.39 = (bf16[768]{0:T(1024)(128)(2,1)S(1)}, bf16[768]{0:T(1024)(128)(2,1)}, u32[]{:S(2)}) copy-start(bf16[768]{0:T(1024)(128)(2,1)} %get-tuple-element.47) | copy-start | bytes 4612
  469.3 244.1 %reduce-scatter.9.cloned.1.call-start = ((), (), s32[]{:S(2)}) async-start(), calls=%async_computation.5 | async-start | bytes 9934848
  502.3 1.3 collective-permute-start.5
  503.6 4.6 collective-permute-start.6
  505.3 22.8 %collective-permute-start.2 = (f32[1,14]{1,0:T(1,128)S(1)}, f32[1,14]{1,0:T(1,128)S(1)}, u32[]{:S(2)}, u32[]{:S(2)}) collective-permute-start(f32[1,14]{1,0:T(1,128)S(1)} %bitcast.259), channel_id=1, source_target_pairs={{0,1},{1,0},{2,3},{3,2},{4,5},{5,4},{6,7},{7,6},{8,9},{9,8},{10,11... | collective-permute-start | bytes 176 | tf_op jit(solution)/shard_map/ppermute | solution.py:28
  508.2 7.6 %collective-permute-start.7 = (f32[152,128]{1,0:T(8,128)S(1)}, f32[152,128]{1,0:T(8,128)S(1)}, u32[]{:S(2)}, u32[]{:S(2)}) collective-permute-start(f32[152,128]{1,0:T(8,128)S(1)} %add.260), channel_id=1, source_target_pairs={{0,8},{2,10},{4,12},{6,14},{8,0},{10,2},{12,4},{14,6},{16,24},{18,... | collective-permute-start | bytes 233480 | tf_op jit(solution)/shard_map/ppermute | solution.py:38
  509.6 30.3 %collective-permute-start.1 = (bf16[512,768]{1,0:T(8,128)(2,1)S(1)}, bf16[512,768]{1,0:T(8,128)(2,1)S(1)}, u32[]{:S(2)}, u32[]{:S(2)}) collective-permute-start(bf16[512,768]{1,0:T(8,128)(2,1)S(1)} %dynamic-slice_bitcast_fusion.2), channel_id=1, source_target_pairs={{0,1},{1,0},{2,3},{3,2},{4,5},{5,4},{6,7},{7,6},{8,9},{9,8},{10,11... | collective-permute-start | bytes 2359304 | tf_op jit(solution)/shard_map/ppermute | solution.py:28
  515.8 8.8 %collective-permute-start.8 = (f32[152,128]{1,0:T(8,128)S(1)}, f32[152,128]{1,0:T(8,128)S(1)}, u32[]{:S(2)}, u32[]{:S(2)}) collective-permute-start(f32[152,128]{1,0:T(8,128)S(1)} %add.261), channel_id=1, source_target_pairs={{0,16},{2,18},{4,20},{6,22},{8,24},{10,26},{12,28},{14,30},{16,0},... | collective-permute-start | bytes 233480 | tf_op jit(solution)/shard_map/ppermute | solution.py:38
  516.4 200.9 %copy-start.1 = (bf16[128,128]{1,0:T(8,128)(2,1)S(1)}, bf16[128,128]{1,0:T(8,128)(2,1)}, u32[]{:S(2)}) copy-start(bf16[128,128]{1,0:T(8,128)(2,1)} %param.46) | copy-start | bytes 98308
  524.7 12.9 %collective-permute-start.9 = (f32[152,128]{1,0:T(8,128)S(1)}, f32[152,128]{1,0:T(8,128)S(1)}, u32[]{:S(2)}, u32[]{:S(2)}) collective-permute-start(f32[152,128]{1,0:T(8,128)S(1)} %add.262), channel_id=1, source_target_pairs={{0,1},{1,0},{2,3},{3,2},{4,5},{5,4},{6,7},{7,6},{8,9},{9,8},{10,11... | collective-permute-start | bytes 233480 | tf_op jit(solution)/shard_map/ppermute | solution.py:38
  527.1 29.1 %collective-permute-start.4 = (bf16[512,768]{1,0:T(8,128)(2,1)}, bf16[512,768]{1,0:T(8,128)(2,1)}, u32[]{:S(2)}, u32[]{:S(2)}) collective-permute-start(bf16[512,768]{1,0:T(8,128)(2,1)} %dynamic-slice_bitcast_fusion), channel_id=1, source_target_pairs={{0,1},{1,0},{2,3},{3,2},{4,5},{5,4},{6,7},{7,6},{8,9},{9,8},{10,11... | collective-permute-start | bytes 2359304 | tf_op jit(solution)/shard_map/ppermute | solution.py:28
  528.1 189.2 %copy-start.69 = (f32[2,14]{1,0:T(2,128)}, f32[2,14]{1,0:T(2,128)S(1)}, u32[]{:S(2)}) copy-start(f32[2,14]{1,0:T(2,128)S(1)} %dynamic_update_slice.20) | copy-start | bytes 340
  540.0 177.4 %copy-start.4 = (bf16[2,512,768]{2,1,0:T(8,128)(2,1)}, bf16[2,512,768]{2,1,0:T(8,128)(2,1)S(1)}, u32[]{:S(2)}) copy-start(bf16[2,512,768]{2,1,0:T(8,128)(2,1)S(1)} %bitcast_dynamic-update-slice_fusion.2) | copy-start | bytes 4718596
  (61 other events, 247.8 us)
Sparse Core Ops, SparseCore 0:
  12.8 66.3 all-gather.2
  82.1 86.0 all-gather.4
  469.4 108.0 reduce-scatter.6
  583.4 129.9 reduce-scatter.8
